TPU v7x, 32 devices: a whole 2x2x4 slice. The times are simulated.
32 devices in a mesh: ctx: 8 (over z, y), fsdp: 4 (over x, core).
Axes of the slice: x: 2, y: 2, z: 4, core: 2. Of those that a mesh axis runs over, the one named last changes fastest.
Arguments:
- tokens: bfloat16 [4, 4096, 1024], P('fsdp', 'ctx'), may hold values from -6 to 6
- block_pos: int32 [4, 16], P('fsdp'), may hold values from 0 to 15, each once within a row
- gain_attn: bfloat16 [1024], P('fsdp'), may hold values from 0.25 to 1.75
- w_query: bfloat16 [1024, 256], P('fsdp'), may hold values from -0.1875 to 0.1875
- w_key: bfloat16 [1024, 256], P('fsdp'), may hold values from -0.1875 to 0.1875
- w_value: bfloat16 [1024, 1024], P('fsdp'), may hold values from -0.1875 to 0.1875
- w_out: bfloat16 [1024, 1024], P('fsdp'), may hold values from -2 to 2
- gain_ffn: bfloat16 [1024], P('fsdp'), may hold values from 0.25 to 1.75
- w_gate: bfloat16 [1024, 2752], P('fsdp'), may hold values from -0.1875 to 0.1875
- w_up: bfloat16 [1024, 2752], P('fsdp'), may hold values from -0.1875 to 0.1875
- w_down: bfloat16 [2752, 1024], P('fsdp'), may hold values from -0.109375 to 0.109375
- cotangent: bfloat16 [4, 4096, 1024], P('fsdp', 'ctx'), may hold values from -6 to 6
Outputs:
- output: bfloat16 [4, 4096, 1024], P('fsdp', 'ctx')
- grad_tokens: float32 [4, 4096, 1024], P('fsdp', 'ctx')
- grad_gain_attn: float32 [1024], P('fsdp')
- grad_query: float32 [1024, 256], P('fsdp')
- grad_key: float32 [1024, 256], P('fsdp')
- grad_value: float32 [1024, 1024], P('fsdp')
- grad_out: float32 [1024, 1024], P('fsdp')
- grad_gain_ffn: float32 [1024], P('fsdp')
- grad_gate: float32 [1024, 2752], P('fsdp')
- grad_up: float32 [1024, 2752], P('fsdp')
- grad_down: float32 [2752, 1024], P('fsdp')
Inputs may be any that keep to these rules, and one draw needn't show every extreme that they name: `block_pos`: each row is a permutation of the 16 position blocks of one sequence.
All inputs are finite; a program needn't handle non-finite values.
Results may differ from a plain program's by a relative error of at most 0.015.
Values may be sent and summed in bfloat16 or wider, within the bound.
A program may use at most 512 MiB of HBM per device.

v0:
```python
import jax
import jax.numpy as jnp
from jax import lax
from jax.sharding import PartitionSpec as P

HEADS = 16
FDIM = 16
VDIM = 64
BLOCK = 256
highest = lax.Precision.HIGHEST
eps_norm = 1e-05
root_half = 0.7071067811865476


def features(scaled):
    outer_prod = scaled[..., :, None] * scaled[..., None, :]
    flattened = (
        outer_prod.reshape(scaled.shape[:-1] + (scaled.shape[-1] * scaled.shape[-1],)) * root_half
    )
    constant = jnp.ones(scaled.shape[:-1] + (1,), jnp.float32)
    return jnp.concatenate([constant, scaled, flattened], axis=-1)


def features_back(scaled, grad_feat):
    feat_dim = scaled.shape[-1]
    linear = grad_feat[..., 1 : 1 + feat_dim]
    square = (
        grad_feat[..., 1 + feat_dim :].reshape(scaled.shape[:-1] + (feat_dim, feat_dim)) * root_half
    )
    return linear + jnp.einsum("...ab,...b->...a", square + jnp.swapaxes(square, -1, -2), scaled)


def norm_forward(values, gain_vector):
    inv_rms = lax.rsqrt(jnp.mean(values * values, axis=-1, keepdims=True) + eps_norm)
    return (values * inv_rms * gain_vector, inv_rms)


def norm_backward(values, inv_rms, gain_vector, grad_normed):
    weighted = grad_normed * gain_vector
    grad_gain = jnp.sum(grad_normed * values * inv_rms, axis=0)
    grad_values = inv_rms * weighted - values * (inv_rms * inv_rms * inv_rms) * jnp.mean(
        weighted * values, axis=-1, keepdims=True
    )
    return (grad_values, grad_gain)


def block_group():
    for group_size in (8, 4, 2):
        return group_size
    return 1


def body(
    tokens,
    block_pos,
    gain_attn,
    w_query,
    w_key,
    w_value,
    w_out,
    gain_ffn,
    w_gate,
    w_up,
    w_down,
    cotangent,
):
    gathered = (
        lax.all_gather(gain_attn, "fsdp", axis=0, tiled=True),
        lax.all_gather(w_query, "fsdp", axis=0, tiled=True),
        lax.all_gather(w_key, "fsdp", axis=0, tiled=True),
        lax.all_gather(w_value, "fsdp", axis=0, tiled=True),
        lax.all_gather(w_out, "fsdp", axis=0, tiled=True),
        lax.all_gather(gain_ffn, "fsdp", axis=0, tiled=True),
        lax.all_gather(w_gate, "fsdp", axis=0, tiled=True),
        lax.all_gather(w_up, "fsdp", axis=0, tiled=True),
        lax.all_gather(w_down, "fsdp", axis=0, tiled=True),
    )
    norm_one_gain = gathered[0].astype(jnp.float32)
    query_full, key_full, value_full, out_full = (
        gathered[1],
        gathered[2],
        gathered[3],
        gathered[4],
    )
    norm_two_gain = gathered[5].astype(jnp.float32)
    gate_full, up_full, down_full = (gathered[6], gathered[7], gathered[8])
    residual = tokens[0].astype(jnp.float32)
    row_count = residual.shape[0]
    local_blocks = row_count // BLOCK
    feat_width = 1 + FDIM + FDIM * FDIM
    positions = block_pos[0]
    own_positions = lax.dynamic_slice_in_dim(
        positions, lax.axis_index("ctx") * local_blocks, local_blocks
    )
    normed_one, inv_rms_one = norm_forward(residual, norm_one_gain)
    normed_one_low = normed_one.astype(jnp.bfloat16)
    queries = jnp.dot(normed_one_low, query_full, preferred_element_type=jnp.float32).astype(
        jnp.bfloat16
    )
    keys_all = jnp.dot(normed_one_low, key_full, preferred_element_type=jnp.float32).astype(
        jnp.bfloat16
    )
    values_all = jnp.dot(normed_one_low, value_full, preferred_element_type=jnp.float32).astype(
        jnp.bfloat16
    )
    query_blocks = queries.reshape(local_blocks, BLOCK, HEADS, FDIM)
    key_blocks = keys_all.reshape(local_blocks, BLOCK, HEADS, FDIM)
    value_blocks = values_all.reshape(local_blocks, BLOCK, HEADS, VDIM)
    query_scaled = query_blocks.astype(jnp.float32) * 0.5
    key_scaled = key_blocks.astype(jnp.float32) * 0.5
    phi_query = features(query_scaled).astype(jnp.bfloat16)
    phi_key = features(key_scaled).astype(jnp.bfloat16)
    state_zero = jnp.zeros((local_blocks, HEADS, feat_width, VDIM), jnp.float32)
    norm_zero = jnp.zeros((local_blocks, HEADS, feat_width), jnp.float32)
    running = (state_zero, norm_zero)
    key_piece = lax.all_gather(keys_all, "ctx", axis=0, tiled=True)
    value_piece = lax.all_gather(values_all, "ctx", axis=0, tiled=True)
    block_count = key_piece.shape[0] // BLOCK
    group_size = block_group()
    others = positions
    key_groups = key_piece.reshape(block_count // group_size, group_size, BLOCK, HEADS, FDIM)
    value_groups = value_piece.reshape(block_count // group_size, group_size, BLOCK, HEADS, VDIM)
    other_groups = others.reshape(block_count // group_size, group_size)

    def one_group(inner_sum, group_args):
        keys_here, values_here, places = group_args
        key_feat = features(keys_here.astype(jnp.float32) * 0.5).astype(jnp.bfloat16)
        states = jnp.einsum(
            "gthf,gthv->ghfv", key_feat, values_here, preferred_element_type=jnp.float32
        )
        norm_sums = jnp.sum(key_feat.astype(jnp.float32), axis=1)
        earlier = (places[None, :] < own_positions[:, None]).astype(jnp.float32)
        return (
            (
                inner_sum[0] + jnp.einsum("ig,ghfv->ihfv", earlier, states, precision=highest),
                inner_sum[1] + jnp.einsum("ig,ghf->ihf", earlier, norm_sums, precision=highest),
            ),
            None,
        )

    running, unused = lax.scan(one_group, running, (key_groups, value_groups, other_groups))
    prefix, prefix_norm = running
    phi_query_wide = phi_query.astype(jnp.float32)
    scores = (
        jnp.einsum("nshf,nthf->nhst", query_blocks, key_blocks, preferred_element_type=jnp.float32)
        * 0.25
    )
    kernel = 1.0 + scores + 0.5 * scores * scores
    kernel_low = kernel.astype(jnp.bfloat16)
    numerator = jnp.einsum(
        "nhst,nthv->nshv", kernel_low, value_blocks, preferred_element_type=jnp.float32
    ) + jnp.einsum("nshf,nhfv->nshv", phi_query_wide, prefix, precision=highest)
    denominator = jnp.transpose(jnp.sum(kernel, axis=-1), (0, 2, 1)) + jnp.einsum(
        "nshf,nhf->nsh", phi_query_wide, prefix_norm, precision=highest
    )
    attention_full = numerator / denominator[..., None]
    attention_low = attention_full.reshape(row_count, HEADS * VDIM).astype(jnp.bfloat16)
    middle = residual + jnp.dot(attention_low, out_full, preferred_element_type=jnp.float32)
    normed_two, inv_rms_two = norm_forward(middle, norm_two_gain)
    normed_two_low = normed_two.astype(jnp.bfloat16)
    gate_pre = jnp.dot(normed_two_low, gate_full, preferred_element_type=jnp.float32)
    up_pre = jnp.dot(normed_two_low, up_full, preferred_element_type=jnp.float32)
    sigmoid_gate = jax.nn.sigmoid(gate_pre)
    silu_gate = gate_pre * sigmoid_gate
    hidden_low = (silu_gate * up_pre).astype(jnp.bfloat16)
    result = middle + jnp.dot(hidden_low, down_full, preferred_element_type=jnp.float32)
    output = result.astype(jnp.bfloat16)[None]
    cotangent_low = cotangent[0]
    grad_out_full = cotangent_low.astype(jnp.float32)
    grad_down_full = jnp.einsum(
        "tf,td->fd", hidden_low, cotangent_low, preferred_element_type=jnp.float32
    )
    grad_hidden = jnp.einsum(
        "td,fd->tf", cotangent_low, down_full, preferred_element_type=jnp.float32
    )
    grad_gate_pre = (
        grad_hidden * up_pre * (sigmoid_gate * (1.0 + gate_pre * (1.0 - sigmoid_gate)))
    ).astype(jnp.bfloat16)
    grad_up_pre = (grad_hidden * silu_gate).astype(jnp.bfloat16)
    grad_gate_full = jnp.einsum(
        "td,tf->df", normed_two_low, grad_gate_pre, preferred_element_type=jnp.float32
    )
    grad_up_full = jnp.einsum(
        "td,tf->df", normed_two_low, grad_up_pre, preferred_element_type=jnp.float32
    )
    grad_normed_two = jnp.einsum(
        "tf,df->td", grad_gate_pre, gate_full, preferred_element_type=jnp.float32
    ) + jnp.einsum("tf,df->td", grad_up_pre, up_full, preferred_element_type=jnp.float32)
    grad_middle_norm, grad_gain_two = norm_backward(
        middle, inv_rms_two, norm_two_gain, grad_normed_two
    )
    grad_middle = grad_out_full + grad_middle_norm
    grad_branch = grad_middle.astype(jnp.bfloat16)
    grad_out_proj = jnp.einsum(
        "ta,td->ad", attention_low, grad_branch, preferred_element_type=jnp.float32
    )
    grad_attention = jnp.einsum(
        "td,ad->ta", grad_branch, out_full, preferred_element_type=jnp.float32
    )
    grad_attention = grad_attention.reshape(local_blocks, BLOCK, HEADS, VDIM)
    grad_numerator = (grad_attention / denominator[..., None]).astype(jnp.bfloat16)
    grad_denominator = (-jnp.sum(grad_attention * attention_full, axis=-1) / denominator).astype(
        jnp.bfloat16
    )
    grad_denom_wide = grad_denominator.astype(jnp.float32)
    grad_kernel = (
        jnp.einsum(
            "nshv,nthv->nhst", grad_numerator, value_blocks, preferred_element_type=jnp.float32
        )
        + jnp.transpose(grad_denom_wide, (0, 2, 1))[..., None]
    )
    grad_scores = ((1.0 + scores) * grad_kernel).astype(jnp.bfloat16)
    flat_numer = grad_numerator.reshape(row_count, HEADS * VDIM)
    flat_denom = grad_denominator.reshape(row_count, HEADS)
    running = (state_zero, norm_zero)
    query_piece = lax.all_gather(queries, "ctx", axis=0, tiled=True)
    numer_piece = lax.all_gather(flat_numer, "ctx", axis=0, tiled=True)
    denom_piece = lax.all_gather(flat_denom, "ctx", axis=0, tiled=True)
    block_count = query_piece.shape[0] // BLOCK
    group_size = block_group()
    others = positions
    query_groups = query_piece.reshape(block_count // group_size, group_size, BLOCK, HEADS, FDIM)
    numer_groups = numer_piece.reshape(block_count // group_size, group_size, BLOCK, HEADS, VDIM)
    denom_groups = denom_piece.reshape(block_count // group_size, group_size, BLOCK, HEADS)
    other_groups = others.reshape(block_count // group_size, group_size)

    def one_group(inner_sum, group_args):
        queries_here, numer_here, denom_here, places = group_args
        query_feat = features(queries_here.astype(jnp.float32) * 0.5).astype(jnp.bfloat16)
        grad_states = jnp.einsum(
            "gthf,gthv->ghfv", query_feat, numer_here, preferred_element_type=jnp.float32
        )
        grad_norms = jnp.einsum(
            "gthf,gth->ghf", query_feat, denom_here, preferred_element_type=jnp.float32
        )
        later_mask = (places[None, :] > own_positions[:, None]).astype(jnp.float32)
        return (
            (
                inner_sum[0]
                + jnp.einsum("ig,ghfv->ihfv", later_mask, grad_states, precision=highest),
                inner_sum[1] + jnp.einsum("ig,ghf->ihf", later_mask, grad_norms, precision=highest),
            ),
            None,
        )

    running, unused = lax.scan(
        one_group, running, (query_groups, numer_groups, denom_groups, other_groups)
    )
    later_states, later_norms = running
    grad_phi_query = (
        jnp.einsum("nshv,nhfv->nshf", grad_numerator.astype(jnp.float32), prefix, precision=highest)
        + grad_denom_wide[..., None] * prefix_norm[:, None, :, :]
    )
    grad_phi_key = (
        jnp.einsum(
            "nthv,nhfv->nthf", value_blocks.astype(jnp.float32), later_states, precision=highest
        )
        + later_norms[:, None, :, :]
    )
    grad_values = jnp.einsum(
        "nhst,nshv->nthv", kernel_low, grad_numerator, preferred_element_type=jnp.float32
    ) + jnp.einsum("nthf,nhfv->nthv", phi_key.astype(jnp.float32), later_states, precision=highest)
    grad_values_low = grad_values.reshape(row_count, HEADS * VDIM).astype(jnp.bfloat16)
    grad_queries = jnp.einsum(
        "nhst,nthf->nshf", grad_scores, key_blocks, preferred_element_type=jnp.float32
    ) * 0.25 + 0.5 * features_back(query_scaled, grad_phi_query)
    grad_queries_low = grad_queries.reshape(row_count, HEADS * FDIM).astype(jnp.bfloat16)
    grad_keys = jnp.einsum(
        "nhst,nshf->nthf", grad_scores, query_blocks, preferred_element_type=jnp.float32
    ) * 0.25 + 0.5 * features_back(key_scaled, grad_phi_key)
    grad_keys_low = grad_keys.reshape(row_count, HEADS * FDIM).astype(jnp.bfloat16)
    grad_query_full = jnp.einsum(
        "td,tk->dk", normed_one_low, grad_queries_low, preferred_element_type=jnp.float32
    )
    grad_key_full = jnp.einsum(
        "td,tk->dk", normed_one_low, grad_keys_low, preferred_element_type=jnp.float32
    )
    grad_value_full = jnp.einsum(
        "td,tk->dk", normed_one_low, grad_values_low, preferred_element_type=jnp.float32
    )
    grad_normed_one = (
        jnp.einsum("tk,dk->td", grad_queries_low, query_full, preferred_element_type=jnp.float32)
        + jnp.einsum("tk,dk->td", grad_keys_low, key_full, preferred_element_type=jnp.float32)
        + jnp.einsum("tk,dk->td", grad_values_low, value_full, preferred_element_type=jnp.float32)
    )
    grad_from_norm, grad_gain_one = norm_backward(
        residual, inv_rms_one, norm_one_gain, grad_normed_one
    )
    grad_tokens = (grad_middle + grad_from_norm)[None]
    shards = (
        lax.psum_scatter(
            grad_gain_one.astype(jnp.bfloat16), "fsdp", scatter_dimension=0, tiled=True
        ).astype(jnp.float32),
        lax.psum_scatter(
            grad_query_full.astype(jnp.bfloat16), "fsdp", scatter_dimension=0, tiled=True
        ).astype(jnp.float32),
        lax.psum_scatter(
            grad_key_full.astype(jnp.bfloat16), "fsdp", scatter_dimension=0, tiled=True
        ).astype(jnp.float32),
        lax.psum_scatter(
            grad_value_full.astype(jnp.bfloat16), "fsdp", scatter_dimension=0, tiled=True
        ).astype(jnp.float32),
        lax.psum_scatter(
            grad_out_proj.astype(jnp.bfloat16), "fsdp", scatter_dimension=0, tiled=True
        ).astype(jnp.float32),
        lax.psum_scatter(
            grad_gain_two.astype(jnp.bfloat16), "fsdp", scatter_dimension=0, tiled=True
        ).astype(jnp.float32),
        lax.psum_scatter(
            grad_gate_full.astype(jnp.bfloat16), "fsdp", scatter_dimension=0, tiled=True
        ).astype(jnp.float32),
        lax.psum_scatter(
            grad_up_full.astype(jnp.bfloat16), "fsdp", scatter_dimension=0, tiled=True
        ).astype(jnp.float32),
        lax.psum_scatter(
            grad_down_full.astype(jnp.bfloat16), "fsdp", scatter_dimension=0, tiled=True
        ).astype(jnp.float32),
    )
    totals = lax.psum(
        (
            shards[0],
            shards[1],
            shards[2],
            shards[3],
            shards[4],
            shards[5],
            shards[6],
            shards[7],
            shards[8],
        ),
        "ctx",
    )
    return (
        output,
        grad_tokens,
        totals[0],
        totals[1],
        totals[2],
        totals[3],
        totals[4],
        totals[5],
        totals[6],
        totals[7],
        totals[8],
    )


def solution(mesh):
    in_specs = (
        P("fsdp", "ctx", None),
        P("fsdp", None),
        P("fsdp"),
        P("fsdp", None),
        P("fsdp", None),
        P("fsdp", None),
        P("fsdp", None),
        P("fsdp"),
        P("fsdp", None),
        P("fsdp", None),
        P("fsdp", None),
        P("fsdp", "ctx", None),
    )
    out_specs = (
        P("fsdp", "ctx", None),
        P("fsdp", "ctx", None),
        P("fsdp"),
        P("fsdp", None),
        P("fsdp", None),
        P("fsdp", None),
        P("fsdp", None),
        P("fsdp"),
        P("fsdp", None),
        P("fsdp", None),
        P("fsdp", None),
    )
    return jax.shard_map(body, mesh=mesh, in_specs=in_specs, out_specs=out_specs, check_vma=False)
```

profile of v0, /device:TPU:0, one launch (start us, length us, event | category | flops | bytes accessed | tf_op | source)
XLA Modules:
  0.0 1292.5 jit_solution(17293718670228395038)
XLA Ops:
  8.6 6.0 all-gather
  16.1 9.3 all_gather.45
  28.8 7.1 all-gather.12.cloned.1.call-done
  42.4 7.3 all_gather.44
  55.7 5.1 all-gather.1
  68.4 5.0 fusion.45
  74.0 4.0 reshape.274
  81.6 7.7 all-gather.14.cloned.1.call-done
  89.3 4.1 copy.109
  96.9 118.5 %all-gather.16.cloned.1.call-done = bf16[4096,1024]{1,0:T(8,128)(2,1)} async-done(((bf16[512,1024]{1,0:T(8,128)(2,1)}), bf16[4096,1024]{1,0:T(8,128)(2,1)}) %all-gather.16.cloned.1.call-update) | async-done | bytes 8388624 | tf_op jit(solution)/shard_map/all_gather | solution.py:117
  215.5 22.2 %reshape.269 = bf16[2,8,256,16,64]{4,3,2,1,0:T(8,128)(2,1)} reshape(bf16[4096,1024]{1,0:T(8,128)(2,1)} %all-gather.16.cloned.1.call-done) | data formatting | bytes 16777216 | tf_op jit(solution)/shard_map/reshape | solution.py:122
  237.7 19.7 %copy.112 = bf16[2,8,256,16,64]{2,4,3,1,0:T(8,128)(2,1)} copy(bf16[2,8,256,16,64]{4,3,2,1,0:T(8,128)(2,1)} %reshape.269) | data formatting | bytes 16777216
  257.4 111.2 %while.26 = (s32[]{:T(128)}, f32[2,16,273,64]{2,0,3,1:T(2,128)S(1)}, f32[2,16,273]{2,0,1:T(2,128)S(1)}, s32[2,8]{1,0:T(2,128)S(1)}, s32[2]{0:T(128)S(1)}, /*inde...) while((s32[]{:T(128)}, ...), condition=%wide.region_3.4_spmd.clone, body=%wide.region_1.3_spmd.clone.sunk | while | flops 1343690752 | bytes 159030480 | solution.py:141
  259.3 5.2 multiply_convert_fusion.11
  264.4 5.8 copy-done
  270.2 8.2 convert_reduce_fusion.2
  278.4 13.8 %fusion.184 = f32[8,16,273,64]{2,3,1,0:T(8,128)} fusion(bf16[8,256,16,256]{1,3,2,0:T(8,128)(2,1)} %bitcast.288, bf16[8,256,16,16]{1,3,2,0:T(8,128)(2,1)} %copy-done.1, bf16[273]{0:T(512)(128)(2,1)S(1)} %pad.clone.2, bf16[2,8,256,16,64]{2,4,3,1,0:T(8,128)(2,1)} %get-tuple-element.396, s32[]{:T(128)S(6)} %copy.272), kind=kOutput, calls=%fused_computation.5.clone.1 | convolution fusion | flops 1198718976 | bytes 30966310 | tf_op jit(solution)/shard_map/while/body/eval_jaxpr/gthf,gthv->ghfv/dot_general | solution.py:128
  292.3 19.9 %select_add_fusion.4 = f32[2,16,273,64]{2,0,3,1:T(2,128)S(1)} fusion(f32[2,16,273,64]{2,0,3,1:T(2,128)S(1)} %get-tuple-element.380, pred[]{:T(512)S(6)} %compare.6, f32[8,16,273,64]{2,3,1,0:T(8,128)} %fusion.184, s32[8]{0:T(128)S(1)} %fusion.185, s32[2]{0:T(128)S(1)} %get-tuple-element.394), kind=kOutput, calls=%fused_computation.9.clone.1 | convolution fusion | flops 54792208 | bytes 13418537 | tf_op jit(solution)/shard_map/while/body/eval_jaxpr/ig,ghfv->ihfv/dot_general | solution.py:135
  314.2 5.2 multiply_convert_fusion.11
  319.4 5.8 copy-done
  325.2 8.2 convert_reduce_fusion.2
  333.4 15.2 %fusion.184 = f32[8,16,273,64]{2,3,1,0:T(8,128)} fusion(bf16[8,256,16,256]{1,3,2,0:T(8,128)(2,1)} %bitcast.288, bf16[8,256,16,16]{1,3,2,0:T(8,128)(2,1)} %copy-done.1, bf16[273]{0:T(512)(128)(2,1)S(1)} %pad.clone.2, bf16[2,8,256,16,64]{2,4,3,1,0:T(8,128)(2,1)} %get-tuple-element.396, s32[]{:T(128)S(6)} %copy.272), kind=kOutput, calls=%fused_computation.5.clone.1 | convolution fusion | flops 1198718976 | bytes 30966310 | tf_op jit(solution)/shard_map/while/body/eval_jaxpr/gthf,gthv->ghfv/dot_general | solution.py:128
  348.6 19.3 %select_add_fusion.4 = f32[2,16,273,64]{2,0,3,1:T(2,128)S(1)} fusion(f32[2,16,273,64]{2,0,3,1:T(2,128)S(1)} %get-tuple-element.380, pred[]{:T(512)S(6)} %compare.6, f32[8,16,273,64]{2,3,1,0:T(8,128)} %fusion.184, s32[8]{0:T(128)S(1)} %fusion.185, s32[2]{0:T(128)S(1)} %get-tuple-element.394), kind=kOutput, calls=%fused_computation.9.clone.1 | convolution fusion | flops 54792208 | bytes 13418537 | tf_op jit(solution)/shard_map/while/body/eval_jaxpr/ig,ghfv->ihfv/dot_general | solution.py:135
  368.6 5.3 fusion.64
  374.0 4.3 fusion.56
  389.7 8.5 fusion.122
  398.3 8.7 fusion.121
  407.0 12.3 multiply_convert_fusion.5
  422.2 4.8 reshape.270
  427.1 6.2 fusion.123
  433.4 6.2 multiply_reduce_fusion
  444.9 4.6 reshape.275
  449.5 4.8 copy.117
  457.8 6.4 bitcast_add_fusion
  464.2 4.9 slice_multiply_fusion.1
  470.3 16.5 %fusion.44 = f32[2,256,16,16]{1,3,2,0:T(8,128)S(1)} fusion(f32[2,256,16,16,16]{1,4,3,2,0:T(8,128)} %bitcast.293, f32[2,256,16,16]{1,3,2,0:T(8,128)S(1)} %copy-done.21), kind=kLoop, calls=%fused_computation.67 | loop fusion | flops 6160384 | bytes 9437184 | tf_op jit(solution)/shard_map/...ab,...b->...a/dot_general | solution.py:30
  486.8 5.7 multiply_convert_fusion.3
  502.1 7.6 convolution_convert_fusion.2
  511.5 6.2 convolution_convert_fusion
  522.8 4.1 copy.129
  530.6 31.4 %all_gather.55 = bf16[4096,16]{0,1:T(8,128)(2,1)S(1)} all-gather(bf16[512,16]{0,1:T(8,128)(2,1)S(1)} %bitcast.321), channel_id=1, replica_groups=mesh['ctx'=8,'fsdp'=4] {'ctx'}, dimensions={0}, use_global_device_ids=true | all-gather | bytes 147456 | tf_op jit(solution)/shard_map/all_gather | solution.py:218
  562.7 4.9 convolution_convert_fusion.1
  569.9 22.2 %reshape.271 = bf16[2,8,256,16,64]{4,3,2,1,0:T(8,128)(2,1)} reshape(bf16[4096,1024]{1,0:T(8,128)(2,1)} %all-gather.28.cloned.1.call-done) | data formatting | bytes 16777216 | tf_op jit(solution)/shard_map/reshape | solution.py:223
  592.1 19.7 %copy.135 = bf16[2,8,256,16,64]{2,4,3,1,0:T(8,128)(2,1)} copy(bf16[2,8,256,16,64]{4,3,2,1,0:T(8,128)(2,1)} %reshape.271) | data formatting | bytes 16777216
  611.7 114.5 %while.27 = (s32[]{:T(128)}, f32[2,16,273,64]{2,0,3,1:T(2,128)S(1)}, f32[2,16,273]{2,0,1:T(2,128)S(1)}, s32[2,8]{1,0:T(2,128)S(1)}, s32[2]{0:T(128)S(1)}, /*inde...) while((s32[]{:T(128)}, ...), condition=%wide.region_9.10_spmd.clone, body=%wide.region_8.9_spmd.clone.sunk | while | flops 1352671360 | bytes 92249264 | solution.py:246
  614.5 8.8 multiply_convert_fusion.12
  623.3 9.2 fusion.193
  632.5 16.2 %fusion.191 = f32[8,16,273,64]{2,3,1,0:T(8,128)} fusion(bf16[8,256,16,256]{1,3,2,0:T(8,128)(2,1)} %bitcast.290, bf16[8,256,16,16]{1,3,2,0:T(8,128)(2,1)} %copy-done.9, bf16[273]{0:T(512)(128)(2,1)S(1)} %pad.3.clone.2, bf16[2,8,256,16,64]{2,4,3,1,0:T(8,128)(2,1)} %get-tuple-element.431, s32[]{:T(128)S(6)} %copy.281), kind=kOutput, calls=%fused_computation.30.clone.1 | convolution fusion | flops 1198718976 | bytes 30966310 | tf_op jit(solution)/shard_map/while/body/eval_jaxpr/gthf,gthv->ghfv/dot_general | solution.py:230
  648.8 19.8 %select_add_fusion.5 = f32[2,16,273,64]{2,0,3,1:T(2,128)S(1)} fusion(f32[2,16,273,64]{2,0,3,1:T(2,128)S(1)} %get-tuple-element.414, pred[]{:T(512)S(6)} %compare.7, f32[8,16,273,64]{2,3,1,0:T(8,128)} %fusion.191, s32[8]{0:T(128)S(1)} %fusion.192, s32[2]{0:T(128)S(1)} %get-tuple-element.429), kind=kOutput, calls=%fused_computation.35.clone.1 | convolution fusion | flops 54792208 | bytes 13418537 | tf_op jit(solution)/shard_map/while/body/eval_jaxpr/ig,ghfv->ihfv/dot_general | solution.py:240
  671.6 8.8 multiply_convert_fusion.12
  680.4 9.3 fusion.193
  689.7 16.1 %fusion.191 = f32[8,16,273,64]{2,3,1,0:T(8,128)} fusion(bf16[8,256,16,256]{1,3,2,0:T(8,128)(2,1)} %bitcast.290, bf16[8,256,16,16]{1,3,2,0:T(8,128)(2,1)} %copy-done.9, bf16[273]{0:T(512)(128)(2,1)S(1)} %pad.3.clone.2, bf16[2,8,256,16,64]{2,4,3,1,0:T(8,128)(2,1)} %get-tuple-element.431, s32[]{:T(128)S(6)} %copy.281), kind=kOutput, calls=%fused_computation.30.clone.1 | convolution fusion | flops 1198718976 | bytes 30966310 | tf_op jit(solution)/shard_map/while/body/eval_jaxpr/gthf,gthv->ghfv/dot_general | solution.py:230
  705.7 19.7 %select_add_fusion.5 = f32[2,16,273,64]{2,0,3,1:T(2,128)S(1)} fusion(f32[2,16,273,64]{2,0,3,1:T(2,128)S(1)} %get-tuple-element.414, pred[]{:T(512)S(6)} %compare.7, f32[8,16,273,64]{2,3,1,0:T(8,128)} %fusion.191, s32[8]{0:T(128)S(1)} %fusion.192, s32[2]{0:T(128)S(1)} %get-tuple-element.429), kind=kOutput, calls=%fused_computation.35.clone.1 | convolution fusion | flops 54792208 | bytes 13418537 | tf_op jit(solution)/shard_map/while/body/eval_jaxpr/ig,ghfv->ihfv/dot_general | solution.py:240
  726.2 6.9 add_bitcast_fusion
  733.2 4.9 slice_multiply_fusion
  739.2 17.3 %fusion.41 = f32[2,256,16,16]{1,3,2,0:T(8,128)} fusion(f32[2,256,16,16,16]{1,4,3,2,0:T(8,128)} %bitcast.294, f32[2,256,16,16]{1,3,2,0:T(8,128)S(1)} %copy-done.23), kind=kLoop, calls=%fused_computation.63 | loop fusion | flops 6160384 | bytes 9437184 | tf_op jit(solution)/shard_map/...ab,...b->...a/dot_general | solution.py:30
  761.8 8.4 fusion.48
  770.3 6.2 fusion.81
  785.7 7.7 fusion.80
  799.4 4.2 fusion.77
  803.5 5.9 all-reduce.3
  813.0 7.9 reduce-scatter.10.cloned.1.call-done
  820.9 34.4 %reduce-scatter.12.cloned.1.call-done = bf16[256,1024]{1,0:T(8,128)(2,1)} async-done(((bf16[1024,1024]{1,0:T(8,128)(2,1)}), bf16[256,1024]{1,0:T(8,128)(2,1)}) %reduce-scatter.12.cloned.1.call-update) | async-done | bytes 524304 | tf_op jit(solution)/shard_map/reduce_scatter | solution.py:300
  855.3 430.5 %all-reduce.5 = (f32[256]{0:T(256)}, f32[256,256]{1,0:T(8,128)}, f32[256,256]{1,0:T(8,128)}, f32[256,1024]{1,0:T(8,128)}, f32[256,1024]{1,0:T(8,128)}, /*index=5...) all-reduce(f32[256]{0:T(256)S(1)} %get-tuple-element.267, ...), channel_id=1, replica_groups=mesh['ctx'=8,'fsdp'=4] {'ctx'}, use_global_device_ids=true, to_apply=%region_13.14 | all-reduce | flops 2769408 | bytes 16617472 | tf_op jit(solution)/shard_map/psum | solution.py:319
  (286 shorter events, 115.7 us)
Async XLA Ops:
  7.2 28.8 %copy-start.11 = (bf16[1,512,1024]{2,1,0:T(8,128)(2,1)S(1)}, bf16[1,512,1024]{2,1,0:T(8,128)(2,1)}, u32[]{:S(2)}) copy-start(bf16[1,512,1024]{2,1,0:T(8,128)(2,1)} %param.16) | copy-start | bytes 3145732
  7.2 28.7 %all-gather.12.cloned.1.call-start = ((), (), s32[]{:S(2)}) async-start(), calls=%async_computation.7 | async-start | bytes 2621440 | tf_op jit(solution)/shard_map/all_gather | solution.py:71
  7.9 81.4 %all-gather.14.cloned.1.call-start = ((), (), s32[]{:S(2)}) async-start(), calls=%async_computation.8 | async-start | bytes 2359296 | tf_op jit(solution)/shard_map/all_gather | solution.py:116
  14.6 35.1 %copy-start.53 = (f32[4,1,256]{2,1,0:T(1,128)}, f32[4,1,256]{2,1,0:T(1,128)S(1)}, u32[]{:S(2)}) copy-start(f32[4,1,256]{2,1,0:T(1,128)S(1)} %convert_element_type.281) | copy-start | bytes 12292
  26.1 23.6 %copy-start.58 = (f32[512]{0:T(512)}, f32[512]{0:T(512)S(1)}, u32[]{:S(2)}) copy-start(f32[512]{0:T(512)S(1)} %get-tuple-element.253) | copy-start | bytes 6148
  28.7 186.7 %all-gather.16.cloned.1.call-start = ((), (), s32[]{:S(2)}) async-start(), calls=%async_computation.9 | async-start | bytes 9437184 | tf_op jit(solution)/shard_map/all_gather | solution.py:117
  39.8 343.9 %all-gather.18.cloned.1.call-start = ((), (), s32[]{:S(2)}) async-start(), calls=%async_computation.10 | async-start | bytes 2621440 | tf_op jit(solution)/shard_map/all_gather | solution.py:72
  40.4 13.2 %copy-start.39 = (bf16[512,256]{1,0:T(8,128)(2,1)S(1)}, bf16[512,256]{1,0:T(8,128)(2,1)}, u32[]{:S(2)}) copy-start(bf16[512,256]{1,0:T(8,128)(2,1)} %convolution_convert_fusion.8) | copy-start | bytes 786436
  40.4 349.3 %all-gather.22.cloned.1.call-start = ((), (), s32[]{:S(2)}) async-start(), calls=%async_computation.12 | async-start | bytes 7045120 | tf_op jit(solution)/shard_map/all_gather | solution.py:75
  41.0 13.4 %copy-start.66 = (s32[1,16]{1,0:T(1,128)S(1)}, s32[1,16]{1,0:T(1,128)}, u32[]{:S(2)}) copy-start(s32[1,16]{1,0:T(1,128)} %param.17) | copy-start | bytes 196
  41.0 14.7 %copy-start.67 = (bf16[256]{0:T(256)(128)(2,1)S(1)}, bf16[256]{0:T(256)(128)(2,1)}, u32[]{:S(2)}) copy-start(bf16[256]{0:T(256)(128)(2,1)} %param.23) | copy-start | bytes 1540
  41.0 357.3 %all-gather.20.cloned.1.call-start = ((), (), s32[]{:S(2)}) async-start(), calls=%async_computation.11 | async-start | bytes 7045120 | tf_op jit(solution)/shard_map/all_gather | solution.py:74
  41.6 365.4 %all-gather.24.cloned.1.call-start = ((), (), s32[]{:S(2)}) async-start(), calls=%async_computation.13 | async-start | bytes 7045120 | tf_op jit(solution)/shard_map/all_gather | solution.py:76
  42.3 480.5 %all-gather.26.cloned.1.call-start = ((), (), s32[]{:S(2)}) async-start(), calls=%async_computation.14 | async-start | bytes 2359296 | tf_op jit(solution)/shard_map/all_gather | solution.py:216
  51.7 518.2 %all-gather.28.cloned.1.call-start = ((), (), s32[]{:S(2)}) async-start(), calls=%async_computation.15 | async-start | bytes 9437184 | tf_op jit(solution)/shard_map/all_gather | solution.py:217
  62.4 11.1 copy-start.28
  65.0 8.5 copy-start.20
  257.3 111.2 %copy-start.64 = (bf16[273]{0:T(512)(128)(2,1)S(1)}, bf16[273]{0:T(512)(128)(2,1)}, u32[]{:S(2)}) copy-start(bf16[273]{0:T(512)(128)(2,1)} %pad.9.clone) | copy-start | bytes 1642
  259.3 5.2 copy-start.1
  264.4 5.8 copy-start
  314.2 5.2 copy-start.1
  319.4 5.8 copy-start
  368.6 5.4 copy-start.45
  368.6 5.3 copy-start.68
  368.6 5.3 copy-start.26
  368.6 5.3 copy-start.44
  368.6 9.7 slice-start
  382.4 6.1 copy-start.50
  387.8 10.4 copy-start.56
  427.1 6.2 copy-start.7
  427.1 6.2 copy-start.24
  427.1 6.2 copy-start.51
  427.1 6.3 copy-start.57
  433.3 6.3 copy-start.36
  433.3 6.3 copy-start.62
  444.8 348.6 %reduce-scatter.8.cloned.1.call-start = ((), (), s32[]{:S(2)}) async-start(), calls=%async_computation.16 | async-start | bytes 655360 | tf_op jit(solution)/shard_map/reduce_scatter | solution.py:294
  457.1 29.7 %copy-start.10 = (bf16[2,256,16,64]{1,3,2,0:T(8,128)(2,1)}, bf16[2,256,16,64]{1,3,2,0:T(8,128)(2,1)S(1)}, u32[]{:S(2)}) copy-start(bf16[2,256,16,64]{1,3,2,0:T(8,128)(2,1)S(1)} %get-tuple-element.246) | copy-start | bytes 3145732
  464.2 6.1 copy-start.4
  464.2 6.1 copy-start.21
  470.3 16.5 %copy-start.16 = (bf16[2,256,16,64]{1,3,2,0:T(8,128)(2,1)S(1)}, bf16[2,256,16,64]{1,3,2,0:T(8,128)(2,1)}, u32[]{:S(2)}) copy-start(bf16[2,256,16,64]{1,3,2,0:T(8,128)(2,1)} %copy.107) | copy-start | bytes 3145732
  486.8 7.8 copy-start.31
  499.4 294.0 %reduce-scatter.14.cloned.1.call-start = ((), (), s32[]{:S(2)}) async-start(), calls=%async_computation.19 | async-start | bytes 2621440 | tf_op jit(solution)/shard_map/reduce_scatter | solution.py:303
  502.1 291.3 %reduce-scatter.20.cloned.1.call-start = ((), (), s32[]{:S(2)}) async-start(), calls=%async_computation.22 | async-start | bytes 7045120 | tf_op jit(solution)/shard_map/reduce_scatter | solution.py:315
  509.7 283.7 %reduce-scatter.18.cloned.1.call-start = ((), (), s32[]{:S(2)}) async-start(), calls=%async_computation.21 | async-start | bytes 7045120 | tf_op jit(solution)/shard_map/reduce_scatter | solution.py:312
  517.7 278.4 %reduce-scatter.16.cloned.1.call-start = ((), (), s32[]{:S(2)}) async-start(), calls=%async_computation.20 | async-start | bytes 7045120 | tf_op jit(solution)/shard_map/reduce_scatter | solution.py:309
  522.8 7.8 copy-start.52
  526.9 35.8 %copy-start.37 = (bf16[512,1024]{1,0:T(8,128)(2,1)S(1)}, bf16[512,1024]{1,0:T(8,128)(2,1)}, u32[]{:S(2)}) copy-start(bf16[512,1024]{1,0:T(8,128)(2,1)} %multiply_convert_fusion.8) | copy-start | bytes 3145732
  526.9 35.8 %copy-start.71 = (bf16[512,2752]{0,1:T(8,128)(2,1)S(1)}, bf16[512,2752]{0,1:T(8,128)(2,1)}, u32[]{:S(2)}) copy-start(bf16[512,2752]{0,1:T(8,128)(2,1)} %get-tuple-element.244) | copy-start | bytes 8454148
  567.6 253.3 %reduce-scatter.10.cloned.1.call-start = ((), (), s32[]{:S(2)}) async-start(), calls=%async_computation.17 | async-start | bytes 655360 | tf_op jit(solution)/shard_map/reduce_scatter | solution.py:297
  592.0 19.7 %copy-start.46 = (s32[2]{0:T(128)S(1)}, s32[2]{0:T(128)}, u32[]{:S(2)}) copy-start(s32[2]{0:T(128)} %copy-done.45) | copy-start | bytes 28
  592.0 19.7 %copy-start.69 = (s32[2,8]{1,0:T(2,128)S(1)}, s32[2,8]{1,0:T(2,128)}, u32[]{:S(2)}) copy-start(s32[2,8]{1,0:T(2,128)} %copy-done.68) | copy-start | bytes 196
  614.5 8.8 copy-start.9
  671.6 8.8 copy-start.9
  733.2 6.0 copy-start.5
  733.2 6.0 copy-start.23
  739.2 17.3 %copy-start.3 = (bf16[2,16,256,256]{2,3,1,0:T(8,128)(2,1)S(1)}, bf16[2,16,256,256]{2,3,1,0:T(8,128)(2,1)}, u32[]{:S(2)}) copy-start(bf16[2,16,256,256]{2,3,1,0:T(8,128)(2,1)} %copy-done.2) | copy-start | bytes 12582916
  739.2 17.3 %copy-start.29 = (bf16[2,256,16,16]{1,0,3,2:T(2,128)(2,1)S(1)}, bf16[2,256,16,16]{1,0,3,2:T(2,128)(2,1)}, u32[]{:S(2)}) copy-start(bf16[2,256,16,16]{1,0,3,2:T(2,128)(2,1)} %copy-done.28) | copy-start | bytes 786436
  756.5 5.3 copy-start.65
  770.2 85.1 %reduce-scatter.12.cloned.1.call-start = ((), (), s32[]{:S(2)}) async-start(), calls=%async_computation.18 | async-start | bytes 2621440 | tf_op jit(solution)/shard_map/reduce_scatter | solution.py:300
  778.8 6.9 copy-start.8
  793.4 5.9 copy-start.43
  799.3 10.2 copy-start.19
  799.4 10.2 copy-start.61
  803.5 51.8 %copy-start.48 = (bf16[256,256]{1,0:T(8,128)(2,1)S(1)}, bf16[256,256]{1,0:T(8,128)(2,1)}, u32[]{:S(2)}) copy-start(bf16[256,256]{1,0:T(8,128)(2,1)} %reduce-scatter.8.cloned.1.call-done) | copy-start | bytes 393220
  (29 other events, 82.8 us)
Sparse Core Ops, SparseCore 0:
  9.6 26.2 all-gather.11
  38.6 50.6 all-gather.13
  92.0 123.4 all-gather.15
  216.9 20.7 all-gather.17
  239.1 43.3 all-gather.21
  283.9 43.3 all-gather.19
  328.9 42.6 all-gather.23
  373.7 49.2 all-gather.25
  444.9 124.8 all-gather.27
  572.2 20.0 reduce-scatter.7
  594.9 31.4 reduce-scatter.13
  628.8 54.0 reduce-scatter.19
  685.6 53.9 reduce-scatter.17
  742.1 54.0 reduce-scatter.15
  799.2 21.6 reduce-scatter.9
  823.8 31.4 reduce-scatter.11
where the time goes:
time: 1300 us; the launch traced here: 1290 us
  blocking collectives  495 us (38%)
  matrix products  317 us (24%)
  waiting for transfers between devices  184 us (14%)
  local copies, waits for them, and re-layouts  168 us (13%)
  other arithmetic  111 us (9%)
  between operations  15.6 us (1%)
    psum x1, blocking collectives, body(): lax.psum((shards[0], shards[1], shards[2], shards[3], shards[4], shards[5...  430 us
    all_gather x1, waiting for transfers between devices, body(): value_piece = lax.all_gather(values_all, 'ctx', axis=0, tiled=True)  119 us
    unnamed x156, local copies, waits for them, and re-layouts  63.5 us
    dot_general x2, matrix products, one_group(): jnp.einsum('ig,ghfv->ihfv', later_mask, grad_states, precision=highest)  39.6 us
    dot_general x2, matrix products, one_group(): jnp.einsum('ig,ghfv->ihfv', earlier, states, precision=highest)  39.2 us
    another operation x12, other arithmetic  37.8 us
    reduce_scatter x1, waiting for transfers between devices, body(): lax.psum_scatter(grad_value_full.astype(jnp.bfloat16), 'fsdp', scatter_di...  34.4 us
    dot_general x2, other arithmetic, features_back(): jnp.einsum('...ab,...b->...a', square + jnp.swapaxes(square, -1, -2), sca...  33.7 us
  transfers between devices with their start and end apart: 16, of which 7 were waited for; matrix products, arithmetic and copies ran while one was open for 44% of the time, Pallas kernels for 0%

commit v1 on v0

--- a/solution.py
+++ b/solution.py
@@ -214,8 +214,14 @@
     flat_denom = grad_denominator.reshape(row_count, HEADS)
     running = (state_zero, norm_zero)
     query_piece = lax.all_gather(queries, "ctx", axis=0, tiled=True)
-    numer_piece = lax.all_gather(flat_numer, "ctx", axis=0, tiled=True)
-    denom_piece = lax.all_gather(flat_denom, "ctx", axis=0, tiled=True)
+    _create_inputs = lambda mine_x, local_array, dev_axis: jnp.split(
+        lax.all_gather(
+            jnp.concatenate([mine_x, local_array], 1), tiled=True, axis=0, axis_name=dev_axis
+        ),
+        [mine_x.shape[1]],
+        1,
+    )
+    numer_piece, denom_piece = _create_inputs(flat_numer, flat_denom, "ctx")
     block_count = query_piece.shape[0] // BLOCK
     group_size = block_group()
     others = positions

time: 1300 us -> 1340 us (1.031)
  waiting for transfers between devices: 184 us -> 227 us
  blocking collectives: 495 us -> 465 us
    all_gather x1, waiting for transfers between devices: 2.24 us -> 58 us  [body(): lax.all_gather(jnp.concatenate([mine_x, local_array], 1), tiled=True, axi...]
    all_gather x1 -> x0, blocking collectives: 31.4 us -> none  [body(): denom_piece = lax.all_gather(flat_denom, 'ctx', axis=0, tiled=True)]
    unnamed x156 -> x146, local copies, waits for them, and re-layouts: 63.5 us -> 65.3 us
  transfers between devices with their start and end apart: 16 -> 16, of which waited for: 7 -> 5; matrix products, arithmetic and copies ran while one was open for 44% -> 45% of each run, Pallas kernels for 0% -> 0%
where the time goes in v1:
time: 1340 us; the launch traced here: 1320 us
  blocking collectives  465 us (35%)
  matrix products  319 us (24%)
  waiting for transfers between devices  227 us (17%)
  local copies, waits for them, and re-layouts  180 us (13%)
  other arithmetic  116 us (9%)
  between operations  15.7 us (1%)
    psum x1, blocking collectives, body(): lax.psum((shards[0], shards[1], shards[2], shards[3], shards[4], shards[5...  430 us
    all_gather x1, waiting for transfers between devices, body(): value_piece = lax.all_gather(values_all, 'ctx', axis=0, tiled=True)  119 us
    unnamed x146, local copies, waits for them, and re-layouts  65.3 us
    all_gather x1, waiting for transfers between devices, body(): lax.all_gather(jnp.concatenate([mine_x, local_array], 1), tiled=True, axi...  58 us
    dot_general x2, matrix products, one_group(): jnp.einsum('ig,ghfv->ihfv', earlier, states, precision=highest)  39.2 us
    dot_general x2, matrix products, one_group(): jnp.einsum('ig,ghfv->ihfv', later_mask, grad_states, precision=highest)  38.7 us
    another operation x12, other arithmetic  37.8 us
    dot_general x2, other arithmetic, features_back(): jnp.einsum('...ab,...b->...a', square + jnp.swapaxes(square, -1, -2), sca...  35.1 us
  transfers between devices with their start and end apart: 16, of which 5 were waited for; matrix products, arithmetic and copies ran while one was open for 45% of the time, Pallas kernels for 0%

profile of v1, /device:TPU:0, one launch (start us, length us, event | category | flops | bytes accessed | tf_op | source)
XLA Modules:
  0.0 1324.2 jit_solution(12932482195734430319)
XLA Ops:
  8.6 6.0 all-gather
  16.1 9.3 all_gather.42
  28.8 7.1 all-gather.12.cloned.1.call-done
  42.4 7.3 all_gather.41
  55.8 5.1 all-gather.1
  68.5 5.0 fusion.45
  81.7 7.6 all-gather.14.cloned.1.call-done
  89.3 4.1 copy.109
  96.9 118.5 %all-gather.16.cloned.1.call-done = bf16[4096,1024]{1,0:T(8,128)(2,1)} async-done(((bf16[512,1024]{1,0:T(8,128)(2,1)}), bf16[4096,1024]{1,0:T(8,128)(2,1)}) %all-gather.16.cloned.1.call-update) | async-done | bytes 8388624 | tf_op jit(solution)/shard_map/all_gather | solution.py:117
  215.5 22.2 %reshape.269 = bf16[2,8,256,16,64]{4,3,2,1,0:T(8,128)(2,1)} reshape(bf16[4096,1024]{1,0:T(8,128)(2,1)} %all-gather.16.cloned.1.call-done) | data formatting | bytes 16777216 | tf_op jit(solution)/shard_map/reshape | solution.py:122
  237.6 19.7 %copy.112 = bf16[2,8,256,16,64]{2,4,3,1,0:T(8,128)(2,1)} copy(bf16[2,8,256,16,64]{4,3,2,1,0:T(8,128)(2,1)} %reshape.269) | data formatting | bytes 16777216
  257.3 111.0 %while.26 = (s32[]{:T(128)}, f32[2,16,273,64]{2,0,3,1:T(2,128)S(1)}, f32[2,16,273]{2,0,1:T(2,128)S(1)}, s32[2,8]{1,0:T(2,128)S(1)}, s32[2]{0:T(128)S(1)}, /*inde...) while((s32[]{:T(128)}, ...), condition=%wide.region_3.4_spmd.clone, body=%wide.region_1.3_spmd.clone.sunk | while | flops 1343690752 | bytes 159030480 | solution.py:141
  259.3 5.2 multiply_convert_fusion.11
  264.4 5.8 copy-done
  270.2 8.2 convert_reduce_fusion.2
  278.4 13.8 %fusion.184 = f32[8,16,273,64]{2,3,1,0:T(8,128)} fusion(bf16[8,256,16,256]{1,3,2,0:T(8,128)(2,1)} %bitcast.282, bf16[8,256,16,16]{1,3,2,0:T(8,128)(2,1)} %copy-done.1, bf16[273]{0:T(512)(128)(2,1)S(1)} %pad.clone.2, bf16[2,8,256,16,64]{2,4,3,1,0:T(8,128)(2,1)} %get-tuple-element.396, s32[]{:T(128)S(6)} %copy.265), kind=kOutput, calls=%fused_computation.5.clone.1 | convolution fusion | flops 1198718976 | bytes 30966310 | tf_op jit(solution)/shard_map/while/body/eval_jaxpr/gthf,gthv->ghfv/dot_general | solution.py:128
  292.2 19.9 %select_add_fusion.4 = f32[2,16,273,64]{2,0,3,1:T(2,128)S(1)} fusion(f32[2,16,273,64]{2,0,3,1:T(2,128)S(1)} %get-tuple-element.380, pred[]{:T(512)S(6)} %compare.6, f32[8,16,273,64]{2,3,1,0:T(8,128)} %fusion.184, s32[8]{0:T(128)S(1)} %fusion.185, s32[2]{0:T(128)S(1)} %get-tuple-element.394), kind=kOutput, calls=%fused_computation.9.clone.1 | convolution fusion | flops 54792208 | bytes 13418537 | tf_op jit(solution)/shard_map/while/body/eval_jaxpr/ig,ghfv->ihfv/dot_general | solution.py:135
  314.2 5.2 multiply_convert_fusion.11
  319.4 5.8 copy-done
  325.2 8.2 convert_reduce_fusion.2
  333.4 15.1 %fusion.184 = f32[8,16,273,64]{2,3,1,0:T(8,128)} fusion(bf16[8,256,16,256]{1,3,2,0:T(8,128)(2,1)} %bitcast.282, bf16[8,256,16,16]{1,3,2,0:T(8,128)(2,1)} %copy-done.1, bf16[273]{0:T(512)(128)(2,1)S(1)} %pad.clone.2, bf16[2,8,256,16,64]{2,4,3,1,0:T(8,128)(2,1)} %get-tuple-element.396, s32[]{:T(128)S(6)} %copy.265), kind=kOutput, calls=%fused_computation.5.clone.1 | convolution fusion | flops 1198718976 | bytes 30966310 | tf_op jit(solution)/shard_map/while/body/eval_jaxpr/gthf,gthv->ghfv/dot_general | solution.py:128
  348.5 19.3 %select_add_fusion.4 = f32[2,16,273,64]{2,0,3,1:T(2,128)S(1)} fusion(f32[2,16,273,64]{2,0,3,1:T(2,128)S(1)} %get-tuple-element.380, pred[]{:T(512)S(6)} %compare.6, f32[8,16,273,64]{2,3,1,0:T(8,128)} %fusion.184, s32[8]{0:T(128)S(1)} %fusion.185, s32[2]{0:T(128)S(1)} %get-tuple-element.394), kind=kOutput, calls=%fused_computation.9.clone.1 | convolution fusion | flops 54792208 | bytes 13418537 | tf_op jit(solution)/shard_map/while/body/eval_jaxpr/ig,ghfv->ihfv/dot_general | solution.py:135
  368.4 5.3 fusion.64
  373.7 5.5 fusion.56
  379.4 7.8 fusion.120
  389.5 4.8 multiply_reduce_fusion.3
  397.5 5.3 reshape.270
  405.6 8.5 fusion.122
  414.1 8.5 fusion.121
  422.7 11.7 multiply_convert_fusion.5
  437.6 6.2 multiply_reduce_fusion
  449.1 4.5 reshape.275
  453.6 4.5 copy.117
  464.5 7.6 bitcast_add_fusion
  472.1 5.0 slice_multiply_fusion.1
  478.2 16.8 %fusion.44 = f32[2,256,16,16]{1,3,2,0:T(8,128)S(1)} fusion(f32[2,256,16,16,16]{1,4,3,2,0:T(8,128)} %bitcast.285, f32[2,256,16,16]{1,3,2,0:T(8,128)S(1)} %copy-done.19), kind=kLoop, calls=%fused_computation.66 | loop fusion | flops 6160384 | bytes 9437184 | tf_op jit(solution)/shard_map/...ab,...b->...a/dot_general | solution.py:30
  495.1 5.4 multiply_convert_fusion.3
  509.8 7.6 convolution_convert_fusion.2
  519.2 6.5 convolution_convert_fusion
  530.8 4.1 copy.129
  538.6 4.9 convolution_convert_fusion.1
  543.5 58.0 %all-gather.28.cloned.1.call-done = bf16[4096,1040]{1,0:T(8,128)(2,1)} async-done(((bf16[512,1040]{1,0:T(8,128)(2,1)}), bf16[4096,1040]{1,0:T(8,128)(2,1)}) %all-gather.28.cloned.1.call-update) | async-done | bytes 8519696 | tf_op jit(solution)/shard_map/all_gather | solution.py:218
  606.0 7.9 split.8
  613.8 22.2 %reshape.271 = bf16[2,8,256,16,64]{4,3,2,1,0:T(8,128)(2,1)} reshape(bf16[4096,1024]{1,0:T(8,128)(2,1)} %split.8) | data formatting | bytes 16777216 | tf_op jit(solution)/shard_map/reshape | solution.py:229
  636.0 19.4 %copy.135 = bf16[2,8,256,16,64]{2,4,3,1,0:T(8,128)(2,1)} copy(bf16[2,8,256,16,64]{4,3,2,1,0:T(8,128)(2,1)} %reshape.271) | data formatting | bytes 16777216
  655.4 112.3 %while.27 = (s32[]{:T(128)}, f32[2,16,273,64]{2,0,3,1:T(2,128)S(1)}, f32[2,16,273]{2,0,1:T(2,128)S(1)}, s32[2,8]{1,0:T(2,128)S(1)}, s32[2]{0:T(128)S(1)}, /*inde...) while((s32[]{:T(128)}, ...), condition=%wide.region_9.10_spmd.clone, body=%wide.region_8.9_spmd.clone.sunk | while | flops 1352671360 | bytes 92118192 | solution.py:252
  658.4 8.7 multiply_convert_fusion.12
  667.2 10.8 fusion.193
  677.9 14.3 %fusion.191 = f32[8,16,273,64]{2,3,1,0:T(8,128)} fusion(bf16[8,256,16,256]{1,3,2,0:T(8,128)(2,1)} %bitcast.284, bf16[8,256,16,16]{1,3,2,0:T(8,128)(2,1)} %copy-done.8, bf16[273]{0:T(512)(128)(2,1)S(1)} %pad.3.clone.2, bf16[2,8,256,16,64]{2,4,3,1,0:T(8,128)(2,1)} %get-tuple-element.431, s32[]{:T(128)S(6)} %copy.274), kind=kOutput, calls=%fused_computation.30.clone.1 | convolution fusion | flops 1198718976 | bytes 30966310 | tf_op jit(solution)/shard_map/while/body/eval_jaxpr/gthf,gthv->ghfv/dot_general | solution.py:236
  692.2 19.3 %select_add_fusion.5 = f32[2,16,273,64]{2,0,3,1:T(2,128)S(1)} fusion(f32[2,16,273,64]{2,0,3,1:T(2,128)S(1)} %get-tuple-element.414, pred[]{:T(512)S(6)} %compare.7, f32[8,16,273,64]{2,3,1,0:T(8,128)} %fusion.191, s32[8]{0:T(128)S(1)} %fusion.192, s32[2]{0:T(128)S(1)} %get-tuple-element.429), kind=kOutput, calls=%fused_computation.35.clone.1 | convolution fusion | flops 54792208 | bytes 13418537 | tf_op jit(solution)/shard_map/while/body/eval_jaxpr/ig,ghfv->ihfv/dot_general | solution.py:246
  714.4 8.7 multiply_convert_fusion.12
  723.2 10.6 fusion.193
  733.8 14.2 %fusion.191 = f32[8,16,273,64]{2,3,1,0:T(8,128)} fusion(bf16[8,256,16,256]{1,3,2,0:T(8,128)(2,1)} %bitcast.284, bf16[8,256,16,16]{1,3,2,0:T(8,128)(2,1)} %copy-done.8, bf16[273]{0:T(512)(128)(2,1)S(1)} %pad.3.clone.2, bf16[2,8,256,16,64]{2,4,3,1,0:T(8,128)(2,1)} %get-tuple-element.431, s32[]{:T(128)S(6)} %copy.274), kind=kOutput, calls=%fused_computation.30.clone.1 | convolution fusion | flops 1198718976 | bytes 30966310 | tf_op jit(solution)/shard_map/while/body/eval_jaxpr/gthf,gthv->ghfv/dot_general | solution.py:236
  747.9 19.4 %select_add_fusion.5 = f32[2,16,273,64]{2,0,3,1:T(2,128)S(1)} fusion(f32[2,16,273,64]{2,0,3,1:T(2,128)S(1)} %get-tuple-element.414, pred[]{:T(512)S(6)} %compare.7, f32[8,16,273,64]{2,3,1,0:T(8,128)} %fusion.191, s32[8]{0:T(128)S(1)} %fusion.192, s32[2]{0:T(128)S(1)} %get-tuple-element.429), kind=kOutput, calls=%fused_computation.35.clone.1 | convolution fusion | flops 54792208 | bytes 13418537 | tf_op jit(solution)/shard_map/while/body/eval_jaxpr/ig,ghfv->ihfv/dot_general | solution.py:246
  767.8 6.9 add_bitcast_fusion
  774.7 4.9 slice_multiply_fusion
  782.2 18.2 %fusion.41 = f32[2,256,16,16]{1,3,2,0:T(8,128)} fusion(f32[2,256,16,16,16]{1,4,3,2,0:T(8,128)} %bitcast.286, f32[2,256,16,16]{1,3,2,0:T(8,128)S(1)} %copy-done.21), kind=kLoop, calls=%fused_computation.62 | loop fusion | flops 6160384 | bytes 9437184 | tf_op jit(solution)/shard_map/...ab,...b->...a/dot_general | solution.py:30
  805.8 7.7 fusion.48
  813.6 6.2 fusion.81
  829.0 7.6 fusion.80
  840.0 4.2 fusion.77
  844.2 6.9 all-reduce.3
  854.7 32.1 %reduce-scatter.12.cloned.1.call-done = bf16[256,1024]{1,0:T(8,128)(2,1)} async-done(((bf16[1024,1024]{1,0:T(8,128)(2,1)}), bf16[256,1024]{1,0:T(8,128)(2,1)}) %reduce-scatter.12.cloned.1.call-update) | async-done | bytes 524304 | tf_op jit(solution)/shard_map/reduce_scatter | solution.py:306
  886.8 430.5 %all-reduce.5 = (f32[256]{0:T(256)}, f32[256,256]{1,0:T(8,128)}, f32[256,256]{1,0:T(8,128)}, f32[256,1024]{1,0:T(8,128)}, f32[256,1024]{1,0:T(8,128)}, /*index=5...) all-reduce(f32[256]{0:T(256)S(1)} %get-tuple-element.267, ...), channel_id=1, replica_groups=mesh['ctx'=8,'fsdp'=4] {'ctx'}, use_global_device_ids=true, to_apply=%region_13.14 | all-reduce | flops 2769408 | bytes 16617472 | tf_op jit(solution)/shard_map/psum | solution.py:325
  (275 shorter events, 119.9 us)
Async XLA Ops:
  7.2 28.8 %copy-start.10 = (bf16[1,512,1024]{2,1,0:T(8,128)(2,1)S(1)}, bf16[1,512,1024]{2,1,0:T(8,128)(2,1)}, u32[]{:S(2)}) copy-start(bf16[1,512,1024]{2,1,0:T(8,128)(2,1)} %param.16) | copy-start | bytes 3145732
  7.2 28.7 %all-gather.12.cloned.1.call-start = ((), (), s32[]{:S(2)}) async-start(), calls=%async_computation.7 | async-start | bytes 2621440 | tf_op jit(solution)/shard_map/all_gather | solution.py:71
  7.9 81.4 %all-gather.14.cloned.1.call-start = ((), (), s32[]{:S(2)}) async-start(), calls=%async_computation.8 | async-start | bytes 2359296 | tf_op jit(solution)/shard_map/all_gather | solution.py:116
  14.6 35.1 %copy-start.49 = (f32[4,1,256]{2,1,0:T(1,128)}, f32[4,1,256]{2,1,0:T(1,128)S(1)}, u32[]{:S(2)}) copy-start(f32[4,1,256]{2,1,0:T(1,128)S(1)} %convert_element_type.281) | copy-start | bytes 12292
  26.1 23.6 %copy-start.53 = (f32[512]{0:T(512)}, f32[512]{0:T(512)S(1)}, u32[]{:S(2)}) copy-start(f32[512]{0:T(512)S(1)} %get-tuple-element.253) | copy-start | bytes 6148
  28.7 186.7 %all-gather.16.cloned.1.call-start = ((), (), s32[]{:S(2)}) async-start(), calls=%async_computation.9 | async-start | bytes 9437184 | tf_op jit(solution)/shard_map/all_gather | solution.py:117
  39.8 349.7 %all-gather.18.cloned.1.call-start = ((), (), s32[]{:S(2)}) async-start(), calls=%async_computation.10 | async-start | bytes 2621440 | tf_op jit(solution)/shard_map/all_gather | solution.py:72
  40.4 13.2 copy-start.37
  40.4 365.2 %all-gather.22.cloned.1.call-start = ((), (), s32[]{:S(2)}) async-start(), calls=%async_computation.12 | async-start | bytes 7045120 | tf_op jit(solution)/shard_map/all_gather | solution.py:75
  41.0 13.4 %copy-start.62 = (s32[1,16]{1,0:T(1,128)S(1)}, s32[1,16]{1,0:T(1,128)}, u32[]{:S(2)}) copy-start(s32[1,16]{1,0:T(1,128)} %param.17) | copy-start | bytes 196
  41.0 14.8 %copy-start.63 = (bf16[256]{0:T(256)(128)(2,1)S(1)}, bf16[256]{0:T(256)(128)(2,1)}, u32[]{:S(2)}) copy-start(bf16[256]{0:T(256)(128)(2,1)} %param.23) | copy-start | bytes 1540
  41.0 373.1 %all-gather.20.cloned.1.call-start = ((), (), s32[]{:S(2)}) async-start(), calls=%async_computation.11 | async-start | bytes 7045120 | tf_op jit(solution)/shard_map/all_gather | solution.py:74
  41.6 381.1 %all-gather.24.cloned.1.call-start = ((), (), s32[]{:S(2)}) async-start(), calls=%async_computation.13 | async-start | bytes 7045120 | tf_op jit(solution)/shard_map/all_gather | solution.py:76
  42.3 488.4 %all-gather.26.cloned.1.call-start = ((), (), s32[]{:S(2)}) async-start(), calls=%async_computation.14 | async-start | bytes 2359296 | tf_op jit(solution)/shard_map/all_gather | solution.py:216
  51.7 549.8 %all-gather.28.cloned.1.call-start = ((), (), s32[]{:S(2)}) async-start(), calls=%async_computation.15 | async-start | bytes 10616832 | tf_op jit(solution)/shard_map/all_gather | solution.py:218
  62.5 11.1 copy-start.26
  64.3 4.2 copy-start.28
  65.1 8.5 copy-start.18
  257.3 111.0 %copy-start.59 = (bf16[273]{0:T(512)(128)(2,1)S(1)}, bf16[273]{0:T(512)(128)(2,1)}, u32[]{:S(2)}) copy-start(bf16[273]{0:T(512)(128)(2,1)} %pad.11.clone) | copy-start | bytes 1642
  259.2 5.2 copy-start.1
  264.4 5.8 copy-start
  314.2 5.2 copy-start.1
  319.4 5.8 copy-start
  368.3 5.3 copy-start.43
  368.4 5.3 copy-start.64
  368.4 5.3 copy-start.24
  368.4 5.3 copy-start.42
  373.7 5.5 copy-start.47
  397.5 5.3 copy-start.48
  397.5 5.3 copy-start.52
  422.7 11.7 copy-start.61
  437.6 6.2 copy-start.34
  437.6 6.2 copy-start.57
  464.4 372.2 %reduce-scatter.8.cloned.1.call-start = ((), (), s32[]{:S(2)}) async-start(), calls=%async_computation.16 | async-start | bytes 655360 | tf_op jit(solution)/shard_map/reduce_scatter | solution.py:300
  472.1 6.1 copy-start.4
  472.1 6.1 copy-start.19
  478.2 16.9 %copy-start.9 = (bf16[2,256,16,64]{1,3,2,0:T(8,128)(2,1)S(1)}, bf16[2,256,16,64]{1,3,2,0:T(8,128)(2,1)}, u32[]{:S(2)}) copy-start(bf16[2,256,16,64]{1,3,2,0:T(8,128)(2,1)} %get-tuple-element.246) | copy-start | bytes 3145732
  478.2 16.9 %copy-start.14 = (bf16[2,256,16,64]{1,3,2,0:T(8,128)(2,1)S(1)}, bf16[2,256,16,64]{1,3,2,0:T(8,128)(2,1)}, u32[]{:S(2)}) copy-start(bf16[2,256,16,64]{1,3,2,0:T(8,128)(2,1)} %copy.107) | copy-start | bytes 3145732
  495.1 7.5 copy-start.29
  502.5 4.6 copy-start.16
  502.6 4.6 copy-start.25
  507.1 329.5 %reduce-scatter.14.cloned.1.call-start = ((), (), s32[]{:S(2)}) async-start(), calls=%async_computation.19 | async-start | bytes 2621440 | tf_op jit(solution)/shard_map/reduce_scatter | solution.py:309
  509.8 326.8 %reduce-scatter.20.cloned.1.call-start = ((), (), s32[]{:S(2)}) async-start(), calls=%async_computation.22 | async-start | bytes 7045120 | tf_op jit(solution)/shard_map/reduce_scatter | solution.py:321
  517.4 319.2 %reduce-scatter.18.cloned.1.call-start = ((), (), s32[]{:S(2)}) async-start(), calls=%async_computation.21 | async-start | bytes 7045120 | tf_op jit(solution)/shard_map/reduce_scatter | solution.py:318
  525.7 311.0 %reduce-scatter.16.cloned.1.call-start = ((), (), s32[]{:S(2)}) async-start(), calls=%async_computation.20 | async-start | bytes 7045120 | tf_op jit(solution)/shard_map/reduce_scatter | solution.py:315
  543.5 311.2 %reduce-scatter.10.cloned.1.call-start = ((), (), s32[]{:S(2)}) async-start(), calls=%async_computation.17 | async-start | bytes 655360 | tf_op jit(solution)/shard_map/reduce_scatter | solution.py:303
  636.0 19.4 %copy-start.44 = (s32[2]{0:T(128)S(1)}, s32[2]{0:T(128)}, u32[]{:S(2)}) copy-start(s32[2]{0:T(128)} %copy-done.43) | copy-start | bytes 28
  636.0 19.4 %copy-start.65 = (s32[2,8]{1,0:T(2,128)S(1)}, s32[2,8]{1,0:T(2,128)}, u32[]{:S(2)}) copy-start(s32[2,8]{1,0:T(2,128)} %copy-done.64) | copy-start | bytes 196
  658.4 8.7 copy-start.8
  714.4 8.7 copy-start.8
  774.7 7.5 copy-start.5
  774.7 7.5 copy-start.21
  782.2 18.2 %copy-start.3 = (bf16[2,16,256,256]{2,3,1,0:T(8,128)(2,1)S(1)}, bf16[2,16,256,256]{2,3,1,0:T(8,128)(2,1)}, u32[]{:S(2)}) copy-start(bf16[2,16,256,256]{2,3,1,0:T(8,128)(2,1)} %copy-done.2) | copy-start | bytes 12582916
  782.2 18.2 %copy-start.27 = (bf16[2,256,16,16]{1,0,3,2:T(2,128)(2,1)S(1)}, bf16[2,256,16,16]{1,0,3,2:T(2,128)(2,1)}, u32[]{:S(2)}) copy-start(bf16[2,256,16,16]{1,0,3,2:T(2,128)(2,1)} %copy-done.26) | copy-start | bytes 786436
  800.4 3.9 copy-start.12
  800.4 3.9 copy-start.51
  800.4 5.3 copy-start.60
  813.5 73.3 %reduce-scatter.12.cloned.1.call-start = ((), (), s32[]{:S(2)}) async-start(), calls=%async_computation.18 | async-start | bytes 2621440 | tf_op jit(solution)/shard_map/reduce_scatter | solution.py:306
  821.1 5.0 copy-start.39
  822.1 6.9 copy-start.7
  840.0 4.2 copy-start.58
  840.0 11.2 copy-start.17
  840.0 11.2 copy-start.56
  844.2 42.6 %copy-start.46 = (bf16[256,256]{1,0:T(8,128)(2,1)S(1)}, bf16[256,256]{1,0:T(8,128)(2,1)}, u32[]{:S(2)}) copy-start(bf16[256,256]{1,0:T(8,128)(2,1)} %reduce-scatter.8.cloned.1.call-done) | copy-start | bytes 393220
  (24 other events, 57.6 us)
Sparse Core Ops, SparseCore 0:
  9.6 26.2 all-gather.11
  38.6 50.6 all-gather.13
  92.0 123.4 all-gather.15
  216.9 20.7 all-gather.17
  239.1 43.3 all-gather.21
  283.9 43.3 all-gather.19
  328.9 42.6 all-gather.23
  373.7 49.2 all-gather.25
  464.5 136.9 all-gather.27
  603.9 19.8 reduce-scatter.7
  626.4 31.4 reduce-scatter.13
  660.3 53.9 reduce-scatter.19
  717.1 53.9 reduce-scatter.17
  773.5 54.0 reduce-scatter.15
  830.6 21.7 reduce-scatter.9
  855.4 31.3 reduce-scatter.11
